TPU v7x, 32 devices: a whole 2x2x4 slice. The times are simulated.
32 devices in a mesh: ctx: 8 (over y, x, core), tp: 4 (over z).
Axes of the slice: x: 2, y: 2, z: 4, core: 2. Of those that a mesh axis runs over, the one named last changes fastest.
Arguments:
- patches: bfloat16 [4096, 1280], P('ctx'), may hold values from -21 to 21
- window_ids: int32 [4096], P('ctx'), may hold values from -1 to 1023, as said below
- positions: int32 [1024], P('ctx'), may hold values from 0 to 8192, as said below
- text_embed: bfloat16 [8192, 8192], P('ctx', 'tp'), may hold values from -6 to 6
- cotangent: bfloat16 [8192, 8192], P('ctx', 'tp'), may hold values from -0.119628906 to 0.119628906
- qkv_weight: bfloat16 [3, 1280, 1280], P(None, None, 'tp'), may hold values from -0.15625 to 0.15625
- out_weight: bfloat16 [1280, 1280], P('tp'), may hold values from -0.15625 to 0.15625
- merger_weight: bfloat16 [5120, 8192], P('ctx', 'tp'), may hold values from -0.078125 to 0.078125
- norm_gain: bfloat16 [8192], P('tp'), may hold values from 0.099609375 to 1.8984375
Outputs:
- normed: bfloat16 [8192, 8192], P('ctx', 'tp')
- merger_grad: float32 [5120, 8192], P('ctx', 'tp')
Inputs may be any that keep to these rules, and one draw needn't show every extreme that they name: `window_ids`: windows are runs of consecutive patch slots of one index of ctx, each of 4 to 64 slots and a multiple of 4; every window id belongs to one index of ctx; the padding slots of an index of ctx come after its live slots and carry -1. Merged slot j of an index of ctx covers its patch slots 4j to 4j+3 and is live exactly when those are; live slots carry distinct positions, dead ones carry 8192. The live slots of one index of ctx name at most 16 positions among the 1024 positions of any one index of ctx.
All inputs are finite; a program needn't handle non-finite values.
Results may differ from a plain program's by a relative error of at most 0.014.
Values may be sent and summed in bfloat16 or wider, within the bound.
No kernel may reach another device: no remote copies, remote signals or barrier semaphores. Data moves between devices by JAX's collectives and lax.ppermute only.
A program may use at most 128 MiB of HBM per device.

v0:
```python
import jax
import jax.numpy as jnp
from jax import lax
from jax.sharding import PartitionSpec as P

D = 8192
HEAD_DIM = 80


def window_attention(patches, window_ids, qkv_weight):
    slot_rows = patches.shape[0]
    projected = [
        jnp.dot(patches, qkv_weight[i], preferred_element_type=jnp.float32).astype(jnp.bfloat16)
        for i in range(3)
    ]
    local_heads = qkv_weight.shape[2] // HEAD_DIM
    queries = projected[0].reshape(slot_rows, local_heads, HEAD_DIM)
    keys_all = projected[1].reshape(slot_rows, local_heads, HEAD_DIM)
    values = projected[2].reshape(slot_rows, local_heads, HEAD_DIM)
    width = min(512, slot_rows)
    factor = 1.0 / HEAD_DIM**0.5

    def one_block(block_index):
        scores = (
            jnp.einsum("qhd,khd->hqk", queries, keys_all, preferred_element_type=jnp.float32)
            * factor
        )
        allowed = (window_ids[:, None] == window_ids[None, :]) & (window_ids[None, :] >= 0)
        scores = jnp.where(allowed[None], scores, jnp.float32(-1e30))
        highest = jnp.max(scores, axis=2, keepdims=True)
        weights = jnp.exp(scores - highest)
        probs = (weights / jnp.sum(weights, axis=2, keepdims=True)).astype(jnp.bfloat16)
        attended = jnp.einsum("hqk,khd->qhd", probs, values, preferred_element_type=jnp.float32)
        return attended.astype(jnp.bfloat16).reshape(width, local_heads * HEAD_DIM)

    blocks = lax.map(one_block, jnp.arange(slot_rows // width, dtype=jnp.int32))
    return blocks.reshape(slot_rows, local_heads * HEAD_DIM)


def contract_rows(left, right):
    return lax.dot_general(
        left, right, (((0,), (0,)), ((), ())), preferred_element_type=jnp.float32
    )


def shards(
    patches,
    window_ids,
    positions,
    text_embed,
    cotangent,
    qkv_weight,
    out_weight,
    merger_weight,
    norm_gain,
):
    ctx_size = lax.axis_size("ctx")
    slots = positions.shape[0]
    tok_rows = text_embed.shape[0]
    bucket_size = slots // ctx_size
    attended = window_attention(patches, window_ids, qkv_weight)
    partial_out = jnp.dot(attended, out_weight, preferred_element_type=jnp.float32)
    summed = lax.psum(partial_out.astype(jnp.bfloat16), "tp").astype(jnp.float32)
    hidden = (patches.astype(jnp.float32) + summed).astype(jnp.bfloat16)
    merged_in = hidden.reshape(slots, 4 * hidden.shape[1])
    columns = lax.all_to_all(merged_in, "ctx", split_axis=1, concat_axis=0, tiled=True)
    chosen = merged_in
    merged = jnp.dot(
        chosen,
        lax.all_gather(merger_weight, "ctx", axis=0, tiled=True),
        preferred_element_type=jnp.float32,
    ).astype(jnp.bfloat16)
    target = positions // tok_rows
    hits = (target[:, None] == jnp.arange(ctx_size, dtype=jnp.int32)[None, :]).astype(jnp.int32)
    ranks = jnp.sum(jnp.cumsum(hits, axis=0) * hits, axis=1) - 1
    bucket = jnp.where(target < ctx_size, target * bucket_size + ranks, -1)
    select = jnp.arange(slots, dtype=jnp.int32)[:, None] == bucket[None, :]
    select_mat = select.astype(jnp.bfloat16)
    outgoing = jnp.dot(select_mat, merged, preferred_element_type=jnp.float32).astype(jnp.bfloat16)
    local_row = positions % tok_rows
    occupied = jnp.any(select, axis=1)
    out_rows = jnp.where(occupied, jnp.sum(jnp.where(select, local_row[None, :], 0), axis=1), -1)
    incoming, in_rows = (
        lax.all_to_all(outgoing, "ctx", split_axis=0, concat_axis=0, tiled=True),
        lax.all_to_all(out_rows, "ctx", split_axis=0, concat_axis=0, tiled=True),
    )
    placed = jnp.arange(tok_rows, dtype=jnp.int32)[:, None] == in_rows[None, :]
    placed_mat = placed.astype(jnp.bfloat16)
    vision = jnp.dot(placed_mat, incoming, preferred_element_type=jnp.float32)
    is_vision = jnp.any(placed, axis=1)
    embedded = jnp.where(is_vision[:, None], vision, text_embed.astype(jnp.float32))
    gain_vec = norm_gain.astype(jnp.float32)[None, :]
    gained = gain_vec * cotangent.astype(jnp.float32)
    squares, inner = lax.psum(
        (jnp.sum(embedded * embedded, axis=1), jnp.sum(embedded * gained, axis=1)), "tp"
    )
    scale = lax.rsqrt(squares / D + 1e-06)[:, None]
    normed = (embedded * scale * gain_vec).astype(jnp.bfloat16)
    d_embed = (scale * gained - embedded * scale**3 * inner[:, None] / D).astype(jnp.bfloat16)
    back_rows = contract_rows(placed_mat, d_embed).astype(jnp.bfloat16)
    returned = lax.all_to_all(back_rows, "ctx", split_axis=0, concat_axis=0, tiled=True)
    d_merged = contract_rows(select_mat, returned).astype(jnp.bfloat16)
    chosen = columns
    merger_grad = contract_rows(chosen, lax.all_gather(d_merged, "ctx", axis=0, tiled=True))
    return (normed, merger_grad)


def solution(mesh):
    in_specs = (
        P("ctx", None),
        P("ctx"),
        P("ctx"),
        P("ctx", "tp"),
        P("ctx", "tp"),
        P(None, None, "tp"),
        P("tp", None),
        P("ctx", "tp"),
        P("tp"),
    )
    out_specs = (P("ctx", "tp"), P("ctx", "tp"))
    return jax.shard_map(shards, mesh=mesh, in_specs=in_specs, out_specs=out_specs, check_vma=False)
```

profile of v0, /device:TPU:0, one launch (start us, length us, event | category | flops | bytes accessed | tf_op | source)
XLA Modules:
  0.0 256.8 jit_solution(3629582103694238064)
XLA Ops:
  8.0 0.0 copy-start
  8.0 0.0 copy-start.2
  8.0 0.0 copy-start.3
  8.0 0.0 all-reduce.3.cloned.1.call-start
  8.1 2.3 convolution_convert_fusion.5
  10.4 2.2 convolution_convert_fusion.4
  12.6 0.0 copy-done.2
  12.6 1.8 convolution_convert_fusion.6
  14.3 0.0 copy-done.3
  14.4 0.2 compare_and_fusion
  14.6 3.8 %fusion.27 = (f32[4,512]{1,0:T(4,128)S(1)}, f32[4,512,512]{1,2,0:T(8,128)}) fusion(pred[512,512]{0,1:T(8,128)(4,1)S(1)} %compare_and_fusion, bf16[512,4,80]{0,2,1:T(8,128)(2,1)S(1)} %bitcast.45, bf16[512,4,80]{0,2,1:T(8,128)(2,1)S(1)} %bitcast.46), kind=kOutput, calls=%fused_computation.59 | convolution fusion | flops 171966976 | bytes 5120000 | tf_op jit(solution)/shard_map/while/body/eval_jaxpr/sub | solution.py:31
  18.4 2.7 %fusion.8 = bf16[4,80,512]{2,1,0:T(8,128)(2,1)S(1)} fusion(bf16[512,4,80]{0,2,1:T(8,128)(2,1)S(1)} %bitcast.44, f32[4,512,512]{1,2,0:T(8,128)} %get-tuple-element.29, f32[4,512]{1,0:T(4,128)S(1)} %get-tuple-element.28), kind=kOutput, calls=%fused_computation.25 | convolution fusion | flops 170033152 | bytes 4857856 | tf_op jit(solution)/shard_map/while/body/eval_jaxpr/hqk,khd->qhd/dot_general | solution.py:33
  21.1 0.0 copy-start.5
  21.1 0.0 copy-done
  21.1 1.9 convolution_convert_fusion
  23.0 0.0 all-reduce.3.cloned.1.call-update
  23.0 0.0 all-gather.3.cloned.1.call-start
  23.1 0.5 all-gather.3.cloned.1.call-update
  23.6 0.0 copy-done.5
  23.7 0.1 fusion.20
  23.7 0.2 reduce_window_sum.11
  23.9 0.2 select_reduce_fusion.1
  24.1 0.1 fusion.21
  24.2 0.1 select_reduce_fusion
  24.4 0.7 select_n.47
  25.0 5.2 %all-to-all-start = ((s32[8,16,1]{1,2,0:T(1,128)}), s32[8,16,1]{1,2,0:T(1,128)S(1)}, u32[]{:S(2)}, u32[]{:S(2)}) async-start(s32[8,16,1]{1,2,0:T(1,128)} %bitcast), calls=%async_computation | async-start | bytes 8192 | tf_op jit(solution)/shard_map/all_to_all | solution.py:85
  30.2 55.8 %all-reduce.3.cloned.1.call-done = bf16[512,1280]{1,0:T(8,128)(2,1)} async-done(((bf16[512,1280]{1,0:T(8,128)(2,1)}), bf16[512,1280]{1,0:T(8,128)(2,1)}) %all-reduce.3.cloned.1.call-update) | async-done | bytes 1310736 | tf_op jit(solution)/shard_map/psum | solution.py:63
  86.0 1.6 add_convert_fusion
  87.6 0.8 reshape.114
  88.5 0.0 copy-start.4
  88.5 47.0 %all-gather.3.cloned.1.call-done = bf16[5120,2048]{1,0:T(8,128)(2,1)} async-done(((bf16[640,2048]{1,0:T(8,128)(2,1)}), bf16[5120,2048]{1,0:T(8,128)(2,1)}) %all-gather.3.cloned.1.call-update) | async-done | bytes 20971536 | tf_op jit(solution)/shard_map/all_gather | solution.py:70
  135.5 10.9 %convolution_convert_fusion.2 = bf16[128,2048]{1,0:T(8,128)(2,1)} fusion(bf16[128,5120]{1,0:T(8,128)(2,1)S(1)} %reshape.114, bf16[5120,2048]{1,0:T(8,128)(2,1)} %all-gather.3.cloned.1.call-done, s32[128]{0:T(128)S(1)} %compare_select_fusion), kind=kOutput, calls=%fused_computation.16 | convolution fusion | flops 2752004096 | bytes 22807040 | tf_op jit(solution)/shard_map/dot_general | solution.py:79
  146.4 0.0 all-to-all-done
  146.4 3.5 %all-to-all-start.1 = ((bf16[8,16,2048]{2,1,0:T(8,128)(2,1)}), bf16[8,16,2048]{2,1,0:T(8,128)(2,1)S(1)}, u32[]{:S(2)}, u32[]{:S(2)}) async-start(bf16[8,16,2048]{2,1,0:T(8,128)(2,1)} %bitcast.9), calls=%async_computation.1 | async-start | bytes 1048576 | tf_op jit(solution)/shard_map/all_to_all | solution.py:84
  149.9 0.0 all-gather.5.cloned.1.call-start
  149.9 0.0 copy-done.4
  150.0 0.5 broadcast.108
  150.5 0.7 reduce.3
  151.1 0.1 eq.74
  151.2 0.2 fusion.15
  151.5 8.1 %all-to-all-done.1 = bf16[8,16,2048]{2,1,0:T(8,128)(2,1)S(1)} async-done(((bf16[8,16,2048]{2,1,0:T(8,128)(2,1)}), bf16[8,16,2048]{2,1,0:T(8,128)(2,1)S(1)}, u32[]{:S(2)}, u32[]{:S(2)}) %all-to-all-start.1) | async-done | bytes 524320 | tf_op jit(solution)/shard_map/all_to_all | solution.py:84
  159.5 7.1 %multiply_reduce_fusion = (f32[1024]{0:T(1024)S(1)}, f32[1024]{0:T(1024)S(1)}, f32[1024,2048]{1,0:T(8,128)}) fusion(bf16[1024,2048]{1,0:T(8,128)(2,1)} %param.13, f32[2048]{0:T(1024)S(1)} %convert_element_type.78, bf16[1024,2048]{1,0:T(8,128)(2,1)} %param.12, bf16[128,2048]{1,0:T(8,128)(2,1)S(1)} %bitcast.42, s32[128]{0:T(128)S(1)} %eq.74, ...), kind=kOutput, calls=%fused_computation.2 | convolution fusion | flops 553777152 | bytes 17319424 | tf_op jit(solution)/shard_map/dot_general | solution.py:89
  166.6 12.0 %all-reduce = (f32[1024]{0:T(1024)S(1)}, f32[1024]{0:T(1024)S(1)}) all-reduce(f32[1024]{0:T(1024)S(1)} %get-tuple-element.15, f32[1024]{0:T(1024)S(1)} %get-tuple-element.14), channel_id=1, replica_groups=mesh['ctx'=8,'tp'=4] {'tp'}, use_global_device_ids=true, to_apply=%region_9.10 | all-reduce | flops 2048 | bytes 16384 | tf_op jit(solution)/shard_map/psum | solution.py:94
  178.6 6.2 %fusion.3 = bf16[128,2048]{1,0:T(8,128)(2,1)S(1)} fusion(f32[1024,2048]{1,0:T(8,128)} %get-tuple-element.30, bf16[1024,2048]{1,0:T(8,128)(2,1)} %param.13, f32[1024]{0:T(1024)S(1)} %get-tuple-element.17, f32[1024]{0:T(1024)S(1)} %get-tuple-element.24, f32[2048]{0:T(1024)S(1)} %convert_element_type.78, f32[1024]{0:T(1024)S(1)} %get-tuple-element.25, ...), kind=kOutput, calls=%fused_computation.14 | convolution fusion | flops 554041344 | bytes 13128192 | tf_op jit(solution)/shard_map/dot_general | solution.py:41
  184.8 12.1 %all_to_all.49 = bf16[8,16,2048]{2,1,0:T(8,128)(2,1)S(1)} all-to-all(bf16[8,16,2048]{2,1,0:T(8,128)(2,1)S(1)} %bitcast.43), channel_id=1, replica_groups=mesh['ctx'=8,'tp'=4] {'ctx'}, dimensions={0} | all-to-all | bytes 1048576 | tf_op jit(solution)/shard_map/all_to_all | solution.py:101
  196.9 1.2 convolution_convert_fusion.1
  198.1 0.0 all-gather.5.cloned.1.call-update
  198.1 0.5 all_to_all.38
  198.6 1.2 copy.19
  199.8 3.6 %all-to-all-start.2 = ((bf16[128,8,640]{2,0,1:T(8,128)(2,1)}), bf16[128,8,640]{2,0,1:T(8,128)(2,1)S(1)}, u32[]{:S(2)}, u32[]{:S(2)}) async-start(bf16[128,8,640]{2,0,1:T(8,128)(2,1)} %copy.19), calls=%async_computation.2 | async-start | bytes 2621440 | tf_op jit(solution)/shard_map/all_to_all | solution.py:66
  203.4 6.2 %multiply_convert_fusion = bf16[1024,2048]{1,0:T(8,128)(2,1)} fusion(f32[1024,2048]{1,0:T(8,128)} %get-tuple-element.30, f32[2048]{0:T(1024)S(1)} %convert_element_type.78, f32[1024]{0:T(1024)S(1)} %get-tuple-element.25), kind=kLoop, calls=%fused_computation.4 | loop fusion | flops 6291456 | bytes 12595200 | tf_op jit(solution)/shard_map/convert_element_type | solution.py:98
  209.6 15.6 %all-to-all-done.2 = bf16[128,8,640]{2,0,1:T(8,128)(2,1)S(1)} async-done(((bf16[128,8,640]{2,0,1:T(8,128)(2,1)}), bf16[128,8,640]{2,0,1:T(8,128)(2,1)S(1)}, u32[]{:S(2)}, u32[]{:S(2)}) %all-to-all-start.2) | async-done | bytes 1310752 | tf_op jit(solution)/shard_map/all_to_all | solution.py:66
  225.2 16.6 %all-gather.5.cloned.1.call-done = bf16[1024,2048]{1,0:T(8,128)(2,1)} async-done(((bf16[128,2048]{1,0:T(8,128)(2,1)}), bf16[1024,2048]{1,0:T(8,128)(2,1)}) %all-gather.5.cloned.1.call-update) | async-done | bytes 4194320 | tf_op jit(solution)/shard_map/all_gather | solution.py:104
  241.8 0.0 copy-start.1
  241.8 7.5 %fusion.28 = f32[640,2048]{1,0:T(8,128)} fusion(bf16[1024,640]{1,0:T(8,128)(2,1)S(1)} %bitcast.41, bf16[1024,2048]{1,0:T(8,128)(2,1)} %all-gather.5.cloned.1.call-done), kind=kOutput, calls=%fused_computation.60 | convolution fusion | flops 2684354560 | bytes 10747904 | tf_op jit(solution)/shard_map/dot_general | solution.py:41
  249.3 0.0 copy-done.1
  (6 shorter events, 0.0 us)
Async XLA Ops:
  8.0 13.1 %copy-start = (bf16[320,1280]{1,0:T(8,128)(2,1)S(1)}, bf16[320,1280]{1,0:T(8,128)(2,1)}, u32[]{:S(2)}) copy-start(bf16[320,1280]{1,0:T(8,128)(2,1)} %param.15) | copy-start | bytes 2457604
  8.0 4.5 %copy-start.2 = (bf16[512,1280]{1,0:T(8,128)(2,1)S(1)}, bf16[512,1280]{1,0:T(8,128)(2,1)}, u32[]{:S(2)}) copy-start(bf16[512,1280]{1,0:T(8,128)(2,1)} %param.9) | copy-start | bytes 3932164
  8.0 6.3 %copy-start.3 = (s32[512]{0:T(512)S(1)}, s32[512]{0:T(512)}, u32[]{:S(2)}) copy-start(s32[512]{0:T(512)} %param.10) | copy-start | bytes 6148
  8.0 78.0 %all-reduce.3.cloned.1.call-start = ((), (), s32[]{:S(2)}) async-start(), calls=%async_computation.4 | async-start | bytes 2621440 | tf_op jit(solution)/shard_map/psum | solution.py:63
  21.1 2.6 copy-start.5
  23.0 112.5 %all-gather.3.cloned.1.call-start = ((), (), s32[]{:S(2)}) async-start(), calls=%async_computation.5 | async-start | bytes 23592960 | tf_op jit(solution)/shard_map/all_gather | solution.py:70
  25.0 121.4 %all-to-all-start = ((s32[8,16,1]{1,2,0:T(1,128)}), s32[8,16,1]{1,2,0:T(1,128)S(1)}, u32[]{:S(2)}, u32[]{:S(2)}) async-start(s32[8,16,1]{1,2,0:T(1,128)} %bitcast), calls=%async_computation | async-start | bytes 8192 | tf_op jit(solution)/shard_map/all_to_all | solution.py:85
  88.5 61.5 %copy-start.4 = (bf16[2048]{0:T(1024)(128)(2,1)S(1)}, bf16[2048]{0:T(1024)(128)(2,1)}, u32[]{:S(2)}) copy-start(bf16[2048]{0:T(1024)(128)(2,1)} %param.17) | copy-start | bytes 12292
  146.4 13.2 %all-to-all-start.1 = ((bf16[8,16,2048]{2,1,0:T(8,128)(2,1)}), bf16[8,16,2048]{2,1,0:T(8,128)(2,1)S(1)}, u32[]{:S(2)}, u32[]{:S(2)}) async-start(bf16[8,16,2048]{2,1,0:T(8,128)(2,1)} %bitcast.9), calls=%async_computation.1 | async-start | bytes 1048576 | tf_op jit(solution)/shard_map/all_to_all | solution.py:84
  149.9 91.9 %all-gather.5.cloned.1.call-start = ((), (), s32[]{:S(2)}) async-start(), calls=%async_computation.6 | async-start | bytes 4718592 | tf_op jit(solution)/shard_map/all_gather | solution.py:104
  199.8 25.4 %all-to-all-start.2 = ((bf16[128,8,640]{2,0,1:T(8,128)(2,1)}), bf16[128,8,640]{2,0,1:T(8,128)(2,1)S(1)}, u32[]{:S(2)}, u32[]{:S(2)}) async-start(bf16[128,8,640]{2,0,1:T(8,128)(2,1)} %copy.19), calls=%async_computation.2 | async-start | bytes 2621440 | tf_op jit(solution)/shard_map/all_to_all | solution.py:66
  241.8 7.6 %copy-start.1 = (bf16[320,1280]{1,0:T(8,128)(2,1)S(1)}, bf16[320,1280]{1,0:T(8,128)(2,1)}, u32[]{:S(2)}) copy-start(bf16[320,1280]{1,0:T(8,128)(2,1)} %param.15) | copy-start | bytes 2457604
Sparse Core Ops, SparseCore 0:
  23.2 62.7 all-reduce.2
Sparse Core Ops, SparseCore 1:
  25.4 110.0 all-gather.2
  198.2 43.5 all-gather.4
where the time goes:
time: 257 us
  waiting for transfers between devices  144 us (56%)
  matrix products  47.5 us (18%)
  blocking collectives  24.1 us (9%)
  between operations  15.7 us (6%)
  starting transfers between devices  12.4 us (5%)
  other arithmetic  9.6 us (4%)
  local copies, waits for them, and re-layouts  3.84 us (1%)
    psum x1, waiting for transfers between devices, shards(): lax.psum(partial_out.astype(jnp.bfloat16), 'tp').astype(jnp.float32)  55.8 us
    all_gather x1, waiting for transfers between devices, shards(): lax.all_gather(merger_weight, 'ctx', axis=0, tiled=True)  47 us
    all_gather x1, waiting for transfers between devices, shards(): lax.all_gather(d_merged, 'ctx', axis=0, tiled=True)  16.6 us
    all_to_all x1, waiting for transfers between devices, shards(): lax.all_to_all(merged_in, 'ctx', split_axis=1, concat_axis=0, tiled=True)  15.6 us
    dot_general x3, matrix products, contract_rows(): lax.dot_general(left, right, (((0,), (0,)), ((), ())), preferred_element_...  14.9 us
    all_to_all x1, blocking collectives, shards(): lax.all_to_all(back_rows, 'ctx', split_axis=0, concat_axis=0, tiled=True)  12.1 us
    psum x1, blocking collectives, shards(): lax.psum((jnp.sum(embedded * embedded, axis=1), jnp.sum(embedded * gained...  12 us
    dot_general x1, matrix products, shards(): jnp.dot(select_mat, merged, preferred_element_type=jnp.float32)  10.9 us
  transfers between devices with their start and end apart: 6, of which 5 were waited for; matrix products, arithmetic and copies ran while one was open for 9% of the time, Pallas kernels for 0%

commit v1 on v0

--- a/solution.py
+++ b/solution.py
@@ -5,6 +5,13 @@
 
 D = 8192
 HEAD_DIM = 80
+
+
+def gather_over(x, axis, dim):
+    size = lax.axis_size(axis)
+    parts = jnp.stack([x for _ in range(size)])
+    parts = lax.all_to_all(parts, axis, split_axis=0, concat_axis=0)
+    return jnp.concatenate(parts, axis=dim)
 
 
 def window_attention(patches, window_ids, qkv_weight):
@@ -66,9 +73,7 @@
     columns = lax.all_to_all(merged_in, "ctx", split_axis=1, concat_axis=0, tiled=True)
     chosen = merged_in
     merged = jnp.dot(
-        chosen,
-        lax.all_gather(merger_weight, "ctx", axis=0, tiled=True),
-        preferred_element_type=jnp.float32,
+        chosen, gather_over(merger_weight, "ctx", 0), preferred_element_type=jnp.float32
     ).astype(jnp.bfloat16)
     target = positions // tok_rows
     hits = (target[:, None] == jnp.arange(ctx_size, dtype=jnp.int32)[None, :]).astype(jnp.int32)

time: 257 us -> 378 us (1.47)
  waiting for transfers between devices: 144 us -> 252 us
  local copies, waits for them, and re-layouts: 3.84 us -> 12.3 us
  starting transfers between devices: 12.4 us -> 17.3 us
    all_to_all x0 -> x1, waiting for transfers between devices: none -> 150 us  [gather_over(): parts = lax.all_to_all(parts, axis, split_axis=0, concat_axis=0)]
    all_gather x1 -> x0, waiting for transfers between devices: 47 us -> none  [shards(): lax.all_gather(merger_weight, 'ctx', axis=0, tiled=True)]
    another operation x0 -> x1, local copies, waits for them, and re-layouts: none -> 8.45 us  [gather_over(): parts = jnp.stack([x for _ in range(size)])]
    all_to_all x0 -> x1, starting transfers between devices: none -> 6.22 us  [gather_over(): parts = lax.all_to_all(parts, axis, split_axis=0, concat_axis=0)]
    psum x1, waiting for transfers between devices: 55.8 us -> 61.9 us  [shards(): lax.psum(partial_out.astype(jnp.bfloat16), 'tp').astype(jnp.float32)]
  transfers between devices with their start and end apart: 6 -> 6, of which waited for: 5 -> 5; matrix products, arithmetic and copies ran while one was open for 9% -> 10% of each run, Pallas kernels for 0% -> 0%
where the time goes in v1:
time: 378 us; the launch traced here: 377 us
  waiting for transfers between devices  252 us (67%)
  matrix products  46.4 us (12%)
  blocking collectives  25.2 us (7%)
  starting transfers between devices  17.3 us (5%)
  between operations  14.3 us (4%)
  local copies, waits for them, and re-layouts  12.3 us (3%)
  other arithmetic  9.6 us (3%)
    all_to_all x1, waiting for transfers between devices, gather_over(): parts = lax.all_to_all(parts, axis, split_axis=0, concat_axis=0)  150 us
    psum x1, waiting for transfers between devices, shards(): lax.psum(partial_out.astype(jnp.bfloat16), 'tp').astype(jnp.float32)  61.9 us
    all_gather x1, waiting for transfers between devices, shards(): lax.all_gather(d_merged, 'ctx', axis=0, tiled=True)  16.5 us
    all_to_all x1, waiting for transfers between devices, shards(): lax.all_to_all(merged_in, 'ctx', split_axis=1, concat_axis=0, tiled=True)  15.8 us
    dot_general x3, matrix products, contract_rows(): lax.dot_general(left, right, (((0,), (0,)), ((), ())), preferred_element_...  14.9 us
    psum x1, blocking collectives, shards(): lax.psum((jnp.sum(embedded * embedded, axis=1), jnp.sum(embedded * gained...  13.1 us
    all_to_all x1, blocking collectives, shards(): lax.all_to_all(back_rows, 'ctx', split_axis=0, concat_axis=0, tiled=True)  12.1 us
    dot_general x1, matrix products, shards(): jnp.dot(select_mat, merged, preferred_element_type=jnp.float32)  10.8 us
  transfers between devices with their start and end apart: 6, of which 5 were waited for; matrix products, arithmetic and copies ran while one was open for 10% of the time, Pallas kernels for 0%

profile of v1, /device:TPU:0, one launch (start us, length us, event | category | flops | bytes accessed | tf_op | source)
XLA Modules:
  0.0 377.1 jit_solution(14064284301120815800)
XLA Ops:
  7.2 0.0 copy-start
  7.2 8.5 %stack.2 = bf16[8,640,2048]{2,1,0:T(8,128)(2,1)} broadcast(bf16[640,2048]{1,0:T(8,128)(2,1)} %param.16), dimensions={1,2} | broadcast | bytes 23592960 | tf_op jit(solution)/shard_map/stack | solution.py:12
  15.6 0.0 copy-start.3
  15.6 0.0 copy-start.2
  15.6 6.2 %all-to-all-start.1 = ((bf16[8,640,2048]{2,1,0:T(8,128)(2,1)}), bf16[8,640,2048]{2,1,0:T(8,128)(2,1)}, u32[]{:S(2)}, u32[]{:S(2)}) async-start(bf16[8,640,2048]{2,1,0:T(8,128)(2,1)} %stack.2), calls=%async_computation.1 | async-start | bytes 41943040 | tf_op jit(solution)/shard_map/all_to_all | solution.py:13
  21.9 0.0 all-reduce.3.cloned.1.call-start
  21.9 0.0 copy-done.3
  21.9 0.2 compare_and_fusion
  22.2 0.0 copy-done.2
  22.2 1.8 convolution_convert_fusion.5
  24.0 1.8 convolution_convert_fusion.4
  25.7 1.8 convolution_convert_fusion.6
  27.5 3.7 fusion.27
  31.3 0.0 copy-start.5
  31.3 2.7 fusion.8
  34.0 0.0 copy-done
  34.0 1.9 convolution_convert_fusion
  35.9 0.0 all-reduce.3.cloned.1.call-update
  35.9 0.0 copy-done.5
  36.0 0.1 fusion.20
  36.0 0.2 reduce_window_sum.11
  36.2 0.2 select_reduce_fusion.1
  36.4 0.1 fusion.21
  36.5 0.1 select_reduce_fusion
  36.6 0.7 select_n.47
  37.3 61.9 %all-reduce.3.cloned.1.call-done = bf16[512,1280]{1,0:T(8,128)(2,1)} async-done(((bf16[512,1280]{1,0:T(8,128)(2,1)}), bf16[512,1280]{1,0:T(8,128)(2,1)}) %all-reduce.3.cloned.1.call-update) | async-done | bytes 1310736 | tf_op jit(solution)/shard_map/psum | solution.py:70
  99.2 1.6 add_convert_fusion
  100.8 0.8 reshape.119
  101.7 149.7 %all-to-all-done.1 = bf16[8,640,2048]{2,1,0:T(8,128)(2,1)} async-done(((bf16[8,640,2048]{2,1,0:T(8,128)(2,1)}), bf16[8,640,2048]{2,1,0:T(8,128)(2,1)}, u32[]{:S(2)}, u32[]{:S(2)}) %all-to-all-start.1) | async-done | bytes 20971552 | tf_op jit(solution)/shard_map/all_to_all | solution.py:13
  251.4 3.3 all-to-all-start
  254.7 0.0 copy-start.4
  254.7 10.8 %convolution_convert_fusion.2 = bf16[128,2048]{1,0:T(8,128)(2,1)} fusion(bf16[128,5120]{1,0:T(8,128)(2,1)S(1)} %reshape.119, bf16[5120,2048]{1,0:T(8,128)(2,1)} %bitcast.9, s32[128]{0:T(128)S(1)} %compare_select_fusion), kind=kOutput, calls=%fused_computation.16 | convolution fusion | flops 2752004096 | bytes 22807040 | tf_op jit(solution)/shard_map/dot_general | solution.py:84
  265.5 0.0 all-to-all-done
  265.5 4.1 %all-to-all-start.2 = ((bf16[8,16,2048]{2,1,0:T(8,128)(2,1)}), bf16[8,16,2048]{2,1,0:T(8,128)(2,1)S(1)}, u32[]{:S(2)}, u32[]{:S(2)}) async-start(bf16[8,16,2048]{2,1,0:T(8,128)(2,1)} %bitcast.10), calls=%async_computation.2 | async-start | bytes 1048576 | tf_op jit(solution)/shard_map/all_to_all | solution.py:89
  269.6 0.0 all-gather.2.cloned.1.call-start
  269.7 0.0 copy-done.4
  269.7 0.5 broadcast.110
  270.2 0.7 reduce.3
  270.9 0.1 eq.74
  271.0 0.2 fusion.15
  271.2 8.2 %all-to-all-done.2 = bf16[8,16,2048]{2,1,0:T(8,128)(2,1)S(1)} async-done(((bf16[8,16,2048]{2,1,0:T(8,128)(2,1)}), bf16[8,16,2048]{2,1,0:T(8,128)(2,1)S(1)}, u32[]{:S(2)}, u32[]{:S(2)}) %all-to-all-start.2) | async-done | bytes 524320 | tf_op jit(solution)/shard_map/all_to_all | solution.py:89
  279.4 7.0 %multiply_reduce_fusion = (f32[1024]{0:T(1024)S(1)}, f32[1024]{0:T(1024)S(1)}, f32[1024,2048]{1,0:T(8,128)}) fusion(bf16[1024,2048]{1,0:T(8,128)(2,1)} %param.13, f32[2048]{0:T(1024)S(1)} %convert_element_type.78, bf16[1024,2048]{1,0:T(8,128)(2,1)} %param.12, bf16[128,2048]{1,0:T(8,128)(2,1)S(1)} %bitcast.43, s32[128]{0:T(128)S(1)} %eq.74, ...), kind=kOutput, calls=%fused_computation.2 | convolution fusion | flops 553777152 | bytes 17319424 | tf_op jit(solution)/shard_map/dot_general | solution.py:94
  286.4 13.1 %all-reduce = (f32[1024]{0:T(1024)S(1)}, f32[1024]{0:T(1024)S(1)}) all-reduce(f32[1024]{0:T(1024)S(1)} %get-tuple-element.15, f32[1024]{0:T(1024)S(1)} %get-tuple-element.14), channel_id=1, replica_groups=mesh['ctx'=8,'tp'=4] {'tp'}, use_global_device_ids=true, to_apply=%region_9.10 | all-reduce | flops 2048 | bytes 16384 | tf_op jit(solution)/shard_map/psum | solution.py:99
  299.5 6.2 %fusion.3 = bf16[128,2048]{1,0:T(8,128)(2,1)S(1)} fusion(f32[1024,2048]{1,0:T(8,128)} %get-tuple-element.30, bf16[1024,2048]{1,0:T(8,128)(2,1)} %param.13, f32[1024]{0:T(1024)S(1)} %get-tuple-element.17, f32[1024]{0:T(1024)S(1)} %get-tuple-element.24, f32[2048]{0:T(1024)S(1)} %convert_element_type.78, f32[1024]{0:T(1024)S(1)} %get-tuple-element.25, ...), kind=kOutput, calls=%fused_computation.14 | convolution fusion | flops 554041344 | bytes 13128192 | tf_op jit(solution)/shard_map/dot_general | solution.py:48
  305.7 12.1 %all_to_all.54 = bf16[8,16,2048]{2,1,0:T(8,128)(2,1)S(1)} all-to-all(bf16[8,16,2048]{2,1,0:T(8,128)(2,1)S(1)} %bitcast.44), channel_id=1, replica_groups=mesh['ctx'=8,'tp'=4] {'ctx'}, dimensions={0} | all-to-all | bytes 1048576 | tf_op jit(solution)/shard_map/all_to_all | solution.py:106
  317.8 1.2 convolution_convert_fusion.1
  319.0 0.0 all-gather.2.cloned.1.call-update
  319.0 0.5 all_to_all.42
  319.5 1.2 copy.19
  320.7 3.6 all-to-all-start.3
  324.3 6.2 %multiply_convert_fusion = bf16[1024,2048]{1,0:T(8,128)(2,1)} fusion(f32[1024,2048]{1,0:T(8,128)} %get-tuple-element.30, f32[2048]{0:T(1024)S(1)} %convert_element_type.78, f32[1024]{0:T(1024)S(1)} %get-tuple-element.25), kind=kLoop, calls=%fused_computation.4 | loop fusion | flops 6291456 | bytes 12595200 | tf_op jit(solution)/shard_map/convert_element_type | solution.py:103
  330.5 15.8 %all-to-all-done.3 = bf16[128,8,640]{2,0,1:T(8,128)(2,1)S(1)} async-done(((bf16[128,8,640]{2,0,1:T(8,128)(2,1)}), bf16[128,8,640]{2,0,1:T(8,128)(2,1)S(1)}, u32[]{:S(2)}, u32[]{:S(2)}) %all-to-all-start.3) | async-done | bytes 1310752 | tf_op jit(solution)/shard_map/all_to_all | solution.py:73
  346.3 16.5 %all-gather.2.cloned.1.call-done = bf16[1024,2048]{1,0:T(8,128)(2,1)} async-done(((bf16[128,2048]{1,0:T(8,128)(2,1)}), bf16[1024,2048]{1,0:T(8,128)(2,1)}) %all-gather.2.cloned.1.call-update) | async-done | bytes 4194320 | tf_op jit(solution)/shard_map/all_gather | solution.py:109
  362.7 0.0 copy-start.1
  362.7 7.5 %fusion.28 = f32[640,2048]{1,0:T(8,128)} fusion(bf16[1024,640]{1,0:T(8,128)(2,1)S(1)} %bitcast.42, bf16[1024,2048]{1,0:T(8,128)(2,1)} %all-gather.2.cloned.1.call-done), kind=kOutput, calls=%fused_computation.60 | convolution fusion | flops 2684354560 | bytes 10747904 | tf_op jit(solution)/shard_map/dot_general | solution.py:48
  370.3 0.0 copy-done.1
  (6 shorter events, 0.0 us)
Async XLA Ops:
  7.2 26.8 %copy-start = (bf16[320,1280]{1,0:T(8,128)(2,1)S(1)}, bf16[320,1280]{1,0:T(8,128)(2,1)}, u32[]{:S(2)}) copy-start(bf16[320,1280]{1,0:T(8,128)(2,1)} %param.15) | copy-start | bytes 2457604
  15.6 6.3 %copy-start.3 = (s32[512]{0:T(512)S(1)}, s32[512]{0:T(512)}, u32[]{:S(2)}) copy-start(s32[512]{0:T(512)} %param.10) | copy-start | bytes 6148
  15.6 6.6 %copy-start.2 = (bf16[512,1280]{1,0:T(8,128)(2,1)S(1)}, bf16[512,1280]{1,0:T(8,128)(2,1)}, u32[]{:S(2)}) copy-start(bf16[512,1280]{1,0:T(8,128)(2,1)} %param.9) | copy-start | bytes 3932164
  15.6 235.7 %all-to-all-start.1 = ((bf16[8,640,2048]{2,1,0:T(8,128)(2,1)}), bf16[8,640,2048]{2,1,0:T(8,128)(2,1)}, u32[]{:S(2)}, u32[]{:S(2)}) async-start(bf16[8,640,2048]{2,1,0:T(8,128)(2,1)} %stack.2), calls=%async_computation.1 | async-start | bytes 41943040 | tf_op jit(solution)/shard_map/all_to_all | solution.py:13
  21.9 77.3 %all-reduce.3.cloned.1.call-start = ((), (), s32[]{:S(2)}) async-start(), calls=%async_computation.5 | async-start | bytes 2621440 | tf_op jit(solution)/shard_map/psum | solution.py:70
  31.3 4.7 %copy-start.5 = (s32[128]{0:T(128)S(1)}, s32[128]{0:T(128)}, u32[]{:S(2)}) copy-start(s32[128]{0:T(128)} %param.11) | copy-start | bytes 1540
  251.4 14.1 %all-to-all-start = ((s32[8,16,1]{1,2,0:T(1,128)}), s32[8,16,1]{1,2,0:T(1,128)S(1)}, u32[]{:S(2)}, u32[]{:S(2)}) async-start(s32[8,16,1]{1,2,0:T(1,128)} %bitcast), calls=%async_computation | async-start | bytes 8192 | tf_op jit(solution)/shard_map/all_to_all | solution.py:90
  254.7 15.0 %copy-start.4 = (bf16[2048]{0:T(1024)(128)(2,1)S(1)}, bf16[2048]{0:T(1024)(128)(2,1)}, u32[]{:S(2)}) copy-start(bf16[2048]{0:T(1024)(128)(2,1)} %param.17) | copy-start | bytes 12292
  265.5 13.8 %all-to-all-start.2 = ((bf16[8,16,2048]{2,1,0:T(8,128)(2,1)}), bf16[8,16,2048]{2,1,0:T(8,128)(2,1)S(1)}, u32[]{:S(2)}, u32[]{:S(2)}) async-start(bf16[8,16,2048]{2,1,0:T(8,128)(2,1)} %bitcast.10), calls=%async_computation.2 | async-start | bytes 1048576 | tf_op jit(solution)/shard_map/all_to_all | solution.py:89
  269.6 93.1 %all-gather.2.cloned.1.call-start = ((), (), s32[]{:S(2)}) async-start(), calls=%async_computation.6 | async-start | bytes 4718592 | tf_op jit(solution)/shard_map/all_gather | solution.py:109
  320.7 25.5 %all-to-all-start.3 = ((bf16[128,8,640]{2,0,1:T(8,128)(2,1)}), bf16[128,8,640]{2,0,1:T(8,128)(2,1)S(1)}, u32[]{:S(2)}, u32[]{:S(2)}) async-start(bf16[128,8,640]{2,0,1:T(8,128)(2,1)} %copy.19), calls=%async_computation.3 | async-start | bytes 2621440 | tf_op jit(solution)/shard_map/all_to_all | solution.py:73
  362.7 7.5 %copy-start.1 = (bf16[320,1280]{1,0:T(8,128)(2,1)S(1)}, bf16[320,1280]{1,0:T(8,128)(2,1)}, u32[]{:S(2)}) copy-start(bf16[320,1280]{1,0:T(8,128)(2,1)} %param.15) | copy-start | bytes 2457604
Sparse Core Ops, SparseCore 0:
  36.0 63.1 all-reduce.2
  319.2 43.5 all-gather.1
